TPU v7x, 32 devices: a whole 2x2x4 slice. The times are simulated.
32 devices in a mesh: row: 8 (over z, x), col: 4 (over y, core).
Axes of the slice: x: 2, y: 2, z: 4, core: 2. Of those that a mesh axis runs over, the one named last changes fastest.
Arguments:
- vectors: float32 [8, 4096], P(None, ('row', 'col')), may hold values from -6 to 6
- values: float32 [512, 16384], P('row', 'col'), may hold values from -1 to 1
- block_rows: int32 [8, 256], P('row', 'col'), may hold values from 0 to 7
- block_cols: int32 [8, 256], P('row', 'col'), may hold values from 0 to 15
- counts: int32 [8, 4], P('row', 'col'), may hold values from 16 to 64, as said below
Outputs:
- product: float32 [8, 4096], P(None, ('row', 'col'))
Inputs may be any that keep to these rules, and one draw needn't show every extreme that they name: counts[r, c] slots of tile (r, c) hold blocks, the others are unused; some tile uses all 64 slots.
All inputs are finite; a program needn't handle non-finite values.
Results may differ from a plain program's by a relative error of at most 0.0003.
Values sent between devices are 32-bit elements; how exact they have to be, the bound alone decides.
No kernel may reach another device: no remote copies, remote signals or barrier semaphores. Data moves between devices by JAX's collectives and lax.ppermute only.
A program may use at most 64 MiB of HBM per device.

v0:
```python
import jax
import jax.numpy as jnp
from jax import lax
from jax.sharding import PartitionSpec as P

BLK = 64


def tile_terms(blocks, rows, cols, count, row_seg, col_seg):
    highest = lax.Precision.HIGHEST
    slots = blocks.shape[0]
    nvec = row_seg.shape[0]
    row_blocks = row_seg.shape[1] // blocks.shape[1]
    col_blocks = col_seg.shape[1] // blocks.shape[1]
    width = blocks.shape[1]
    live = (jnp.arange(slots, dtype=jnp.int32) < count).astype(jnp.float32)
    row_hits = (rows[:, None] == jnp.arange(row_blocks, dtype=jnp.int32)[None, :]).astype(
        jnp.float32
    ) * live[:, None]
    col_hits = (cols[:, None] == jnp.arange(col_blocks, dtype=jnp.int32)[None, :]).astype(
        jnp.float32
    ) * live[:, None]
    row_parts = row_seg.reshape(nvec, row_blocks, width)
    col_parts = col_seg.reshape(nvec, col_blocks, width)
    col_pick = jnp.take(col_parts, cols, axis=1)
    row_pick = jnp.take(row_parts, rows, axis=1)
    plain = jnp.einsum("kij,vkj->vki", blocks, col_pick, precision=highest)
    turned = jnp.einsum("kji,vkj->vki", blocks, row_pick, precision=highest)
    plain_part = jnp.einsum("kb,vki->vbi", row_hits, plain, precision=highest).reshape(
        nvec, row_blocks * width
    )
    turned_part = jnp.einsum("kb,vki->vbi", col_hits, turned, precision=highest).reshape(
        nvec, col_blocks * width
    )
    return (plain_part, turned_part)


def sum_rows(plain_part):
    return lax.psum_scatter(plain_part, "col", scatter_dimension=1, tiled=True)


def sum_columns(turned_part):
    return lax.psum_scatter(turned_part, "row", scatter_dimension=1, tiled=True)


def per_device(vectors, values, block_rows, block_cols, counts):
    row_seg = lax.all_gather(vectors, "col", axis=1, tiled=True)
    col_seg = lax.all_gather(vectors, "row", axis=1, tiled=True)
    blocks = values.reshape(values.shape[0], BLK, BLK)
    rows = block_rows[0]
    cols = block_cols[0]
    count = counts[0, 0]
    plain_part, turned_part = tile_terms(blocks, rows, cols, count, row_seg, col_seg)
    plain_sum = sum_rows(plain_part)
    turned_sum = sum_columns(turned_part)
    return plain_sum + turned_sum


def solution(mesh):
    in_specs = (
        P(None, ("row", "col")),
        P("row", "col"),
        P("row", "col"),
        P("row", "col"),
        P("row", "col"),
    )
    out_specs = P(None, ("row", "col"))
    return jax.shard_map(
        per_device, mesh=mesh, in_specs=in_specs, out_specs=out_specs, check_vma=False
    )
```

profile of v0, /device:TPU:0, one launch (start us, length us, event | category | flops | bytes accessed | tf_op | source)
XLA Modules:
  0.0 134.8 jit_solution(16836529348863672988)
XLA Ops:
  6.5 0.0 copy-start
  6.5 0.0 reduce-scatter.3.cloned.1.call-start
  6.5 0.7 fusion.20
  7.2 0.7 compare_and_fusion.1
  7.9 2.0 %reshape.91 = f32[64,64,64]{2,1,0:T(8,128)S(1)} reshape(f32[64,4096]{1,0:T(8,128)} %param.6) | data formatting | bytes 2097152 | tf_op jit(solution)/shard_map/reshape | solution.py:49
  9.9 0.0 copy-done
  9.9 0.0 copy-start.1
  9.9 32.4 %all_gather.6 = f32[8,1024]{1,0:T(8,128)S(1)} all-gather(f32[8,128]{1,0:T(8,128)S(1)} %copy-done), channel_id=1, replica_groups=mesh['row'=8,'col'=4] {'row'}, dimensions={1}, use_global_device_ids=true | all-gather | bytes 36864 | tf_op jit(solution)/shard_map/all_gather | solution.py:48
  42.3 0.1 reshape.90
  43.1 0.6 gather_fusion
  43.7 3.4 %convolution_bitcast_fusion.1 = f32[8,64,64]{2,0,1:T(8,128)S(1)} fusion(f32[64,64,64]{2,1,0:T(8,128)S(1)} %reshape.91, f32[64,8,64]{2,1,0:T(8,128)S(1)} %gather_fusion, pred[64]{0:T(512)(128)(4,1)S(1)} %compare_and_fusion.1), kind=kOutput, calls=%fused_computation.3 | convolution fusion | flops 25198592 | bytes 1310784 | tf_op jit(solution)/shard_map/kij,vkj->vki/dot_general | solution.py:27
  47.1 0.0 copy-start.2
  47.2 0.0 copy-done.1
  47.2 0.3 convolution_bitcast_fusion.3
  47.4 0.7 reshape.92
  48.1 0.0 reduce-scatter.3.cloned.1.call-update
  48.1 0.0 reduce-scatter.5.cloned.1.call-start
  48.2 5.2 %all_gather.7 = f32[8,512]{1,0:T(8,128)S(1)} all-gather(f32[8,128]{1,0:T(8,128)S(1)} %copy-done), channel_id=1, replica_groups=mesh['row'=8,'col'=4] {'col'}, dimensions={1}, use_global_device_ids=true | all-gather | bytes 20480 | tf_op jit(solution)/shard_map/all_gather | solution.py:47
  53.4 0.1 reshape.93
  53.5 0.6 gather_fusion.1
  54.1 1.9 %convolution_bitcast_fusion = f32[8,64,64]{2,0,1:T(8,128)S(1)} fusion(f32[64,64,64]{2,1,0:T(8,128)S(1)} %reshape.91, f32[64,8,64]{2,1,0:T(8,128)S(1)} %gather_fusion.1, pred[64]{0:T(512)(128)(4,1)S(1)} %compare_and_fusion), kind=kOutput, calls=%fused_computation.2 | convolution fusion | flops 25198592 | bytes 1310784 | tf_op jit(solution)/shard_map/kji,vkj->vki/dot_general | solution.py:28
  56.1 0.0 copy-done.2
  56.1 0.3 convolution_bitcast_fusion.2
  56.3 0.7 reshape.94
  57.0 0.0 reduce-scatter.5.cloned.1.call-update
  57.0 11.7 %reduce-scatter.3.cloned.1.call-done = f32[8,128]{1,0:T(8,128)} async-done(((f32[8,512]{1,0:T(8,128)}), f32[8,128]{1,0:T(8,128)}) %reduce-scatter.3.cloned.1.call-update) | async-done | bytes 4112 | tf_op jit(solution)/shard_map/reduce_scatter | solution.py:39
  68.7 57.9 %reduce-scatter.5.cloned.1.call-done = f32[8,128]{1,0:T(8,128)} async-done(((f32[8,1024]{1,0:T(8,128)}), f32[8,128]{1,0:T(8,128)}) %reduce-scatter.5.cloned.1.call-update) | async-done | bytes 4112 | tf_op jit(solution)/shard_map/reduce_scatter | solution.py:43
  126.6 1.3 add.57
  (7 shorter events, 0.1 us)
Async XLA Ops:
  6.5 3.3 %copy-start = (f32[8,128]{1,0:T(8,128)S(1)}, f32[8,128]{1,0:T(8,128)}, u32[]{:S(2)}) copy-start(f32[8,128]{1,0:T(8,128)} %param.5) | copy-start | bytes 12292
  6.5 62.2 %reduce-scatter.3.cloned.1.call-start = ((), (), s32[]{:S(2)}) async-start(), calls=%async_computation.2 | async-start | bytes 20480 | tf_op jit(solution)/shard_map/reduce_scatter | solution.py:39
  9.9 37.3 %copy-start.1 = (s32[1,64]{1,0:T(1,128)S(1)}, s32[1,64]{1,0:T(1,128)}, u32[]{:S(2)}) copy-start(s32[1,64]{1,0:T(1,128)} %param.7) | copy-start | bytes 772
  47.1 8.9 %copy-start.2 = (s32[1,64]{1,0:T(1,128)S(1)}, s32[1,64]{1,0:T(1,128)}, u32[]{:S(2)}) copy-start(s32[1,64]{1,0:T(1,128)} %param.8) | copy-start | bytes 772
  48.1 78.5 %reduce-scatter.5.cloned.1.call-start = ((), (), s32[]{:S(2)}) async-start(), calls=%async_computation.3 | async-start | bytes 36864 | tf_op jit(solution)/shard_map/reduce_scatter | solution.py:43
Sparse Core Ops, SparseCore 0:
  48.3 20.4 reduce-scatter.2
  71.9 54.7 reduce-scatter.4
where the time goes:
time: 135 us
  waiting for transfers between devices  69.6 us (52%)
  blocking collectives  37.6 us (28%)
  between operations  14.1 us (10%)
  matrix products  5.88 us (4%)
  local copies, waits for them, and re-layouts  4.82 us (4%)
  other arithmetic  2.63 us (2%)
    reduce_scatter x1, waiting for transfers between devices, sum_columns(): return lax.psum_scatter(turned_part, 'row', scatter_dimension=1, tiled=True)  57.9 us
    all_gather x1, blocking collectives, per_device(): col_seg = lax.all_gather(vectors, 'row', axis=1, tiled=True)  32.4 us
    reduce_scatter x1, waiting for transfers between devices, sum_rows(): return lax.psum_scatter(plain_part, 'col', scatter_dimension=1, tiled=True)  11.7 us
    all_gather x1, blocking collectives, per_device(): row_seg = lax.all_gather(vectors, 'col', axis=1, tiled=True)  5.21 us
    dot_general x1, matrix products, tile_terms(): plain = jnp.einsum('kij,vkj->vki', blocks, col_pick, precision=highest)  3.41 us
  transfers between devices with their start and end apart: 2, of which 2 were waited for; matrix products, arithmetic and copies ran while one was open for 3% of the time, Pallas kernels for 0%

commit v1 on v0

--- a/solution.py
+++ b/solution.py
@@ -45,7 +45,12 @@
 
 def per_device(vectors, values, block_rows, block_cols, counts):
     row_seg = lax.all_gather(vectors, "col", axis=1, tiled=True)
-    col_seg = lax.all_gather(vectors, "row", axis=1, tiled=True)
+    ring = [vectors]
+    for hop in range(7):
+        ring.append(lax.ppermute(ring[-1], "row", [(dev, (dev + 1) % 8) for dev in range(8)]))
+    col_seg = jnp.roll(
+        jnp.concatenate(ring[::-1], axis=1), (lax.axis_index("row") + 1) * ring[0].shape[1], axis=1
+    )
     blocks = values.reshape(values.shape[0], BLK, BLK)
     rows = block_rows[0]
     cols = block_cols[0]

time: 135 us -> 141 us (1.044)
  waiting for transfers between devices: 69.6 us -> 104 us
  blocking collectives: 37.6 us -> 5.19 us
  starting transfers between devices: 0.04 us -> 4.31 us
    all_gather x1 -> x0, blocking collectives: 32.4 us -> none  [per_device(): col_seg = lax.all_gather(vectors, 'row', axis=1, tiled=True)]
    ppermute x0 -> x7, waiting for transfers between devices: none -> 29.5 us  [per_device(): lax.ppermute(ring[-1], 'row', [(dev, (dev + 1) % 8) for dev in range(8)])]
    reduce_scatter x1, waiting for transfers between devices: 11.7 us -> 16.1 us  [sum_rows(): return lax.psum_scatter(plain_part, 'col', scatter_dimension=1, tiled=True)]
    ppermute x0 -> x7, starting transfers between devices: none -> 4.27 us  [per_device(): lax.ppermute(ring[-1], 'row', [(dev, (dev + 1) % 8) for dev in range(8)])]
  transfers between devices with their start and end apart: 2 -> 9, of which waited for: 2 -> 9; matrix products, arithmetic and copies ran while one was open for 3% -> 5% of each run, Pallas kernels for 0% -> 0%
where the time goes in v1:
time: 141 us
  waiting for transfers between devices  104 us (74%)
  between operations  14.2 us (10%)
  matrix products  5.89 us (4%)
  blocking collectives  5.19 us (4%)
  local copies, waits for them, and re-layouts  4.89 us (3%)
  starting transfers between devices  4.31 us (3%)
  other arithmetic  2.62 us (2%)
    reduce_scatter x1, waiting for transfers between devices, sum_columns(): return lax.psum_scatter(turned_part, 'row', scatter_dimension=1, tiled=True)  57.9 us
    ppermute x7, waiting for transfers between devices, per_device(): lax.ppermute(ring[-1], 'row', [(dev, (dev + 1) % 8) for dev in range(8)])  29.5 us
    reduce_scatter x1, waiting for transfers between devices, sum_rows(): return lax.psum_scatter(plain_part, 'col', scatter_dimension=1, tiled=True)  16.1 us
    all_gather x1, blocking collectives, per_device(): row_seg = lax.all_gather(vectors, 'col', axis=1, tiled=True)  5.19 us
    ppermute x7, starting transfers between devices, per_device(): lax.ppermute(ring[-1], 'row', [(dev, (dev + 1) % 8) for dev in range(8)])  4.27 us
    dot_general x1, matrix products, tile_terms(): plain = jnp.einsum('kij,vkj->vki', blocks, col_pick, precision=highest)  3.41 us
  transfers between devices with their start and end apart: 9, of which 9 were waited for; matrix products, arithmetic and copies ran while one was open for 5% of the time, Pallas kernels for 0%

profile of v1, /device:TPU:0, one launch (start us, length us, event | category | flops | bytes accessed | tf_op | source)
XLA Modules:
  0.0 140.6 jit_solution(4016944540735201439)
XLA Ops:
  6.5 0.0 copy-start
  6.5 0.0 reduce-scatter.3.cloned.1.call-start
  6.5 3.0 %collective-permute-start = (f32[8,128]{1,0:T(8,128)}, f32[8,128]{1,0:T(8,128)S(1)}, u32[]{:S(2)}, u32[]{:S(2)}) collective-permute-start(f32[8,128]{1,0:T(8,128)} %param.5), channel_id=1, source_target_pairs={{0,4},{4,8},{8,12},{12,16},{16,20},{20,24},{24,28},{28,0},{1,5},{5... | collective-permute-start | bytes 12296 | tf_op jit(solution)/shard_map/ppermute | solution.py:50
  9.5 0.7 fusion.21
  10.2 0.7 compare_and_fusion
  10.8 2.0 %reshape.91 = f32[64,64,64]{2,1,0:T(8,128)S(1)} reshape(f32[64,4096]{1,0:T(8,128)} %param.6) | data formatting | bytes 2097152 | tf_op jit(solution)/shard_map/reshape | solution.py:54
  12.8 0.0 copy-start.2
  12.9 1.5 %collective-permute-done = f32[8,128]{1,0:T(8,128)S(1)} collective-permute-done((f32[8,128]{1,0:T(8,128)}, f32[8,128]{1,0:T(8,128)S(1)}, u32[]{:S(2)}, u32[]{:S(2)}) %collective-permute-start) | collective-permute-done | bytes 4128 | tf_op jit(solution)/shard_map/ppermute | solution.py:50
  14.4 0.1 collective-permute-start.1
  14.5 0.0 copy-done
  14.5 5.2 %all_gather.3 = f32[8,512]{1,0:T(8,128)S(1)} all-gather(f32[8,128]{1,0:T(8,128)S(1)} %copy-done), channel_id=1, replica_groups=mesh['row'=8,'col'=4] {'col'}, dimensions={1}, use_global_device_ids=true | all-gather | bytes 20480 | tf_op jit(solution)/shard_map/all_gather | solution.py:47
  19.7 0.1 reshape.93
  19.7 0.6 gather_fusion.1
  20.4 0.3 collective-permute-done.1
  20.7 1.2 collective-permute-start.2
  21.9 1.9 %convolution_bitcast_fusion = f32[8,64,64]{2,0,1:T(8,128)S(1)} fusion(f32[64,64,64]{2,1,0:T(8,128)S(1)} %reshape.91, f32[64,8,64]{2,1,0:T(8,128)S(1)} %gather_fusion.1, pred[64]{0:T(512)(128)(4,1)S(1)} %compare_and_fusion), kind=kOutput, calls=%fused_computation.2 | convolution fusion | flops 25198592 | bytes 1310784 | tf_op jit(solution)/shard_map/kji,vkj->vki/dot_general | solution.py:28
  23.9 0.0 copy-start.1
  23.9 3.1 %collective-permute-done.2 = f32[8,128]{1,0:T(8,128)S(1)} collective-permute-done((f32[8,128]{1,0:T(8,128)S(1)}, f32[8,128]{1,0:T(8,128)S(1)}, u32[]{:S(2)}, u32[]{:S(2)}) %collective-permute-start.2) | collective-permute-done | bytes 4128 | tf_op jit(solution)/shard_map/ppermute | solution.py:50
  27.0 0.0 collective-permute-start.3
  27.0 0.0 copy-done.2
  27.0 6.3 %collective-permute-done.3 = f32[8,128]{1,0:T(8,128)S(1)} collective-permute-done((f32[8,128]{1,0:T(8,128)S(1)}, f32[8,128]{1,0:T(8,128)S(1)}, u32[]{:S(2)}, u32[]{:S(2)}) %collective-permute-start.3) | collective-permute-done | bytes 4128 | tf_op jit(solution)/shard_map/ppermute | solution.py:50
  33.3 0.0 collective-permute-start.4
  33.3 6.3 %collective-permute-done.4 = f32[8,128]{1,0:T(8,128)S(1)} collective-permute-done((f32[8,128]{1,0:T(8,128)S(1)}, f32[8,128]{1,0:T(8,128)S(1)}, u32[]{:S(2)}, u32[]{:S(2)}) %collective-permute-start.4) | collective-permute-done | bytes 4128 | tf_op jit(solution)/shard_map/ppermute | solution.py:50
  39.6 0.0 collective-permute-start.5
  40.3 5.6 %collective-permute-done.5 = f32[8,128]{1,0:T(8,128)S(1)} collective-permute-done((f32[8,128]{1,0:T(8,128)S(1)}, f32[8,128]{1,0:T(8,128)S(1)}, u32[]{:S(2)}, u32[]{:S(2)}) %collective-permute-start.5) | collective-permute-done | bytes 4128 | tf_op jit(solution)/shard_map/ppermute | solution.py:50
  45.9 0.0 collective-permute-start.6
  45.9 6.3 %collective-permute-done.6 = f32[8,128]{1,0:T(8,128)S(1)} collective-permute-done((f32[8,128]{1,0:T(8,128)S(1)}, f32[8,128]{1,0:T(8,128)S(1)}, u32[]{:S(2)}, u32[]{:S(2)}) %collective-permute-start.6) | collective-permute-done | bytes 4128 | tf_op jit(solution)/shard_map/ppermute | solution.py:50
  52.4 0.1 reshape.90
  52.5 0.6 gather_fusion
  53.1 3.4 %convolution_bitcast_fusion.1 = f32[8,64,64]{2,0,1:T(8,128)S(1)} fusion(f32[64,64,64]{2,1,0:T(8,128)S(1)} %reshape.91, f32[64,8,64]{2,1,0:T(8,128)S(1)} %gather_fusion, pred[64]{0:T(512)(128)(4,1)S(1)} %compare_and_fusion.1), kind=kOutput, calls=%fused_computation.3 | convolution fusion | flops 25198592 | bytes 1310784 | tf_op jit(solution)/shard_map/kij,vkj->vki/dot_general | solution.py:27
  56.6 0.0 copy-done.1
  56.6 0.3 convolution_bitcast_fusion.3
  56.8 0.7 reshape.92
  57.5 0.0 reduce-scatter.3.cloned.1.call-update
  57.5 0.0 reduce-scatter.5.cloned.1.call-start
  57.6 0.3 convolution_bitcast_fusion.2
  57.9 0.7 reshape.94
  58.6 0.0 reduce-scatter.5.cloned.1.call-update
  58.6 16.1 %reduce-scatter.3.cloned.1.call-done = f32[8,128]{1,0:T(8,128)} async-done(((f32[8,512]{1,0:T(8,128)}), f32[8,128]{1,0:T(8,128)}) %reduce-scatter.3.cloned.1.call-update) | async-done | bytes 4112 | tf_op jit(solution)/shard_map/reduce_scatter | solution.py:39
  74.7 57.9 %reduce-scatter.5.cloned.1.call-done = f32[8,128]{1,0:T(8,128)} async-done(((f32[8,1024]{1,0:T(8,128)}), f32[8,128]{1,0:T(8,128)}) %reduce-scatter.5.cloned.1.call-update) | async-done | bytes 4112 | tf_op jit(solution)/shard_map/reduce_scatter | solution.py:43
  132.5 1.3 add.73
  (24 shorter events, 0.1 us)
Async XLA Ops:
  6.5 7.9 %copy-start = (f32[8,128]{1,0:T(8,128)S(1)}, f32[8,128]{1,0:T(8,128)}, u32[]{:S(2)}) copy-start(f32[8,128]{1,0:T(8,128)} %param.5) | copy-start | bytes 12292
  6.5 68.1 %reduce-scatter.3.cloned.1.call-start = ((), (), s32[]{:S(2)}) async-start(), calls=%async_computation.2 | async-start | bytes 20480 | tf_op jit(solution)/shard_map/reduce_scatter | solution.py:39
  6.5 7.9 %collective-permute-start = (f32[8,128]{1,0:T(8,128)}, f32[8,128]{1,0:T(8,128)S(1)}, u32[]{:S(2)}, u32[]{:S(2)}) collective-permute-start(f32[8,128]{1,0:T(8,128)} %param.5), channel_id=1, source_target_pairs={{0,4},{4,8},{8,12},{12,16},{16,20},{20,24},{24,28},{28,0},{1,5},{5... | collective-permute-start | bytes 12296 | tf_op jit(solution)/shard_map/ppermute | solution.py:50
  12.8 14.2 %copy-start.2 = (s32[1,64]{1,0:T(1,128)S(1)}, s32[1,64]{1,0:T(1,128)}, u32[]{:S(2)}) copy-start(s32[1,64]{1,0:T(1,128)} %param.8) | copy-start | bytes 772
  14.4 6.3 %collective-permute-start.1 = (f32[8,128]{1,0:T(8,128)S(1)}, f32[8,128]{1,0:T(8,128)S(1)}, u32[]{:S(2)}, u32[]{:S(2)}) collective-permute-start(f32[8,128]{1,0:T(8,128)S(1)} %collective-permute-done), channel_id=1, source_target_pairs={{0,4},{4,8},{8,12},{12,16},{16,20},{20,24},{24,28},{28,0},{1,5},{5... | collective-permute-start | bytes 12296 | tf_op jit(solution)/shard_map/ppermute | solution.py:50
  20.7 6.3 %collective-permute-start.2 = (f32[8,128]{1,0:T(8,128)S(1)}, f32[8,128]{1,0:T(8,128)S(1)}, u32[]{:S(2)}, u32[]{:S(2)}) collective-permute-start(f32[8,128]{1,0:T(8,128)S(1)} %collective-permute-done.1), channel_id=1, source_target_pairs={{0,4},{4,8},{8,12},{12,16},{16,20},{20,24},{24,28},{28,0},{1,5},{5... | collective-permute-start | bytes 12296 | tf_op jit(solution)/shard_map/ppermute | solution.py:50
  23.9 32.7 %copy-start.1 = (s32[1,64]{1,0:T(1,128)S(1)}, s32[1,64]{1,0:T(1,128)}, u32[]{:S(2)}) copy-start(s32[1,64]{1,0:T(1,128)} %param.7) | copy-start | bytes 772
  27.0 6.3 %collective-permute-start.3 = (f32[8,128]{1,0:T(8,128)S(1)}, f32[8,128]{1,0:T(8,128)S(1)}, u32[]{:S(2)}, u32[]{:S(2)}) collective-permute-start(f32[8,128]{1,0:T(8,128)S(1)} %collective-permute-done.2), channel_id=1, source_target_pairs={{0,4},{4,8},{8,12},{12,16},{16,20},{20,24},{24,28},{28,0},{1,5},{5... | collective-permute-start | bytes 12296 | tf_op jit(solution)/shard_map/ppermute | solution.py:50
  33.3 6.3 %collective-permute-start.4 = (f32[8,128]{1,0:T(8,128)S(1)}, f32[8,128]{1,0:T(8,128)S(1)}, u32[]{:S(2)}, u32[]{:S(2)}) collective-permute-start(f32[8,128]{1,0:T(8,128)S(1)} %collective-permute-done.3), channel_id=1, source_target_pairs={{0,4},{4,8},{8,12},{12,16},{16,20},{20,24},{24,28},{28,0},{1,5},{5... | collective-permute-start | bytes 12296 | tf_op jit(solution)/shard_map/ppermute | solution.py:50
  39.6 6.3 %collective-permute-start.5 = (f32[8,128]{1,0:T(8,128)S(1)}, f32[8,128]{1,0:T(8,128)S(1)}, u32[]{:S(2)}, u32[]{:S(2)}) collective-permute-start(f32[8,128]{1,0:T(8,128)S(1)} %collective-permute-done.4), channel_id=1, source_target_pairs={{0,4},{4,8},{8,12},{12,16},{16,20},{20,24},{24,28},{28,0},{1,5},{5... | collective-permute-start | bytes 12296 | tf_op jit(solution)/shard_map/ppermute | solution.py:50
  45.9 6.3 %collective-permute-start.6 = (f32[8,128]{1,0:T(8,128)S(1)}, f32[8,128]{1,0:T(8,128)S(1)}, u32[]{:S(2)}, u32[]{:S(2)}) collective-permute-start(f32[8,128]{1,0:T(8,128)S(1)} %collective-permute-done.5), channel_id=1, source_target_pairs={{0,4},{4,8},{8,12},{12,16},{16,20},{20,24},{24,28},{28,0},{1,5},{5... | collective-permute-start | bytes 12296 | tf_op jit(solution)/shard_map/ppermute | solution.py:50
  57.5 75.0 %reduce-scatter.5.cloned.1.call-start = ((), (), s32[]{:S(2)}) async-start(), calls=%async_computation.3 | async-start | bytes 36864 | tf_op jit(solution)/shard_map/reduce_scatter | solution.py:43
Sparse Core Ops, SparseCore 0:
  57.7 16.9 reduce-scatter.2
  77.8 54.6 reduce-scatter.4
